TPU v7x, 32 devices: a whole 2x2x4 slice. The times are simulated.
32 devices in a mesh: section: 2 (over core), blk: 8 (over z, y), head: 2 (over x).
Axes of the slice: x: 2, y: 2, z: 4, core: 2. Of those that a mesh axis runs over, the one named last changes fastest.
Arguments:
- projected: bfloat16 [8192, 8192], P(('section', 'blk')), may hold values from -6 to 6
- key_weight: bfloat16 [8192, 1024], P(None, 'head'), may hold values from -0.0625 to 0.0625
- value_weight: bfloat16 [8192, 1024], P(None, 'head'), may hold values from -0.0625 to 0.0625
- key_gain: float32 [128], replicated, may hold values from 0.1 to 1.9
- queries: bfloat16 [1024, 8, 1024], P('blk', 'section', 'head'), may hold values from -320 to 320
- frame_tokens: int32 [32], replicated, may hold values from 1 to 512, 8192 in all
- span_first: int32 [1024], replicated, may hold values from 0 to 31
- span_count: int32 [1024], replicated, may hold values from 1 to 32
Outputs:
- attended: bfloat16 [1024, 8, 1024], P('blk', 'section', 'head')
Inputs may be any that keep to these rules, and one draw needn't show every extreme that they name: Frame f holds frame_tokens[f] consecutive visual tokens, and they sum to 8192.
All inputs are finite; a program needn't handle non-finite values.
Results may differ from a plain program's by a relative error of at most 0.005.
The roundings to bfloat16 on the way count: a program that leaves them out, or rounds other values in their place, can miss the bound.
Values may be sent and summed in bfloat16 or wider, within the bound.
No kernel may reach another device: no remote copies, remote signals or barrier semaphores. Data moves between devices by JAX's collectives and lax.ppermute only.
A program may use at most 192 MiB of HBM per device.

v0:
```python
import jax
import jax.numpy as jnp
from jax import lax
from jax.sharding import PartitionSpec as P

HD = 128
FRAMES = 32


def span_bounds(frame_tokens, span_first, span_count):
    frame_ids = jnp.arange(FRAMES, dtype=jnp.int32)
    span_end = jnp.minimum(span_first + span_count, FRAMES)
    first_token = jnp.sum(
        jnp.where(frame_ids[None, :] < span_first[:, None], frame_tokens[None, :], 0), axis=1
    )
    end_token = jnp.sum(
        jnp.where(frame_ids[None, :] < span_end[:, None], frame_tokens[None, :], 0), axis=1
    )
    return (first_token, end_token)


def make_tables(projected, key_weight, value_weight, key_gain):
    count_rows = projected.shape[0]
    local_heads = key_weight.shape[1] // HD
    key_raw = jnp.dot(projected, key_weight, preferred_element_type=jnp.float32).reshape(
        count_rows, local_heads, HD
    )
    mean_square = jnp.mean(key_raw * key_raw, axis=2, keepdims=True)
    key_block = (key_raw / jnp.sqrt(mean_square + 1e-05) * key_gain).astype(jnp.bfloat16)
    value_block = (
        jnp.dot(projected, value_weight, preferred_element_type=jnp.float32)
        .astype(jnp.bfloat16)
        .reshape(count_rows, local_heads, HD)
    )
    return (key_block, value_block)


def masked_scores(query_block, key_block, key_positions, first_token, end_token):
    scores = jnp.einsum(
        "npgd,mgd->gnpm", query_block, key_block, preferred_element_type=jnp.float32
    ) * HD ** (-0.5)
    allowed = (key_positions[None, :] >= first_token[:, None]) & (
        key_positions[None, :] < end_token[:, None]
    )
    return jnp.where(allowed[None, :, None, :], scores, -1e30)


def weighted_sum(scores, row_max, value_block):
    weights = jnp.exp(scores - row_max[..., None])
    denominator = jnp.sum(weights, axis=3)
    numerator = jnp.einsum(
        "gnpm,mgd->npgd",
        weights.astype(jnp.bfloat16),
        value_block,
        preferred_element_type=jnp.float32,
    )
    return (numerator, jnp.transpose(denominator, (1, 2, 0)))


def body(
    projected, key_weight, value_weight, key_gain, queries, frame_tokens, span_first, span_count
):
    key_block, value_block = make_tables(projected, key_weight, value_weight, key_gain)
    first_token, end_token = span_bounds(frame_tokens, span_first, span_count)
    own_rows = queries.shape[0]
    sub_heads = queries.shape[1]
    local_heads = key_block.shape[1]
    count_rows = key_block.shape[0]
    section_count = lax.axis_size("section")
    block_count = lax.axis_size("blk")
    block_index = lax.axis_index("blk")
    section_ids = jnp.arange(section_count, dtype=jnp.int32)
    row_ids = jnp.arange(count_rows, dtype=jnp.int32)
    pair_keys, pair_values = (
        lax.all_gather(key_block, "section", axis=0, tiled=True),
        lax.all_gather(value_block, "section", axis=0, tiled=True),
    )
    all_keys, all_values = (
        lax.all_gather(pair_keys, "blk", axis=0, tiled=True),
        lax.all_gather(pair_values, "blk", axis=0, tiled=True),
    )
    block_ids = jnp.arange(block_count, dtype=jnp.int32)
    key_positions = (
        (section_ids[None, :, None] * block_count + block_ids[:, None, None]) * count_rows
        + row_ids[None, None, :]
    ).reshape(-1)
    own_first = lax.dynamic_slice_in_dim(first_token, block_index * own_rows, own_rows)
    own_end = lax.dynamic_slice_in_dim(end_token, block_index * own_rows, own_rows)
    shaped = queries.reshape(own_rows, sub_heads, local_heads, HD)
    scores = masked_scores(shaped, all_keys, key_positions, own_first, own_end)
    row_max = jnp.max(scores, axis=3)
    numerator, denominator = weighted_sum(scores, row_max, all_values)
    attended = numerator / denominator[..., None]
    return attended.astype(jnp.bfloat16).reshape(own_rows, sub_heads, local_heads * HD)


def solution(mesh):
    placed = (
        P(("section", "blk"), None),
        P(None, "head"),
        P(None, "head"),
        P(),
        P("blk", "section", "head"),
        P(),
        P(),
        P(),
    )
    return jax.shard_map(
        body, mesh=mesh, in_specs=placed, out_specs=P("blk", "section", "head"), check_vma=False
    )
```

profile of v0, /device:TPU:0, one launch (start us, length us, event | category | flops | bytes accessed | tf_op | source)
XLA Modules:
  0.0 328.6 jit_solution(8229665058144376835)
XLA Ops:
  6.5 0.0 copy-start.3
  6.5 0.0 all-gather.9.cloned.1.call-start
  6.5 9.5 %multiply_reduce_fusion = (f32[512,4]{0,1:T(4,128)S(1)}, f32[512,512]{0,1:T(8,128)S(1)}) fusion(bf16[512,8192]{1,0:T(8,128)(2,1)} %param.8, bf16[8192,512]{1,0:T(8,128)(2,1)} %param.9), kind=kOutput, calls=%fused_computation.16 | convolution fusion | flops 4295489536 | bytes 17833984 | tf_op jit(solution)/shard_map/dot_general | solution.py:25
  16.0 0.3 copy.17
  16.4 0.0 copy-done.3
  16.4 1.1 multiply_convert_fusion
  17.5 0.0 all-gather.9.cloned.1.call-update
  17.5 0.0 copy-start.1
  17.6 0.0 copy-start.2
  17.6 0.0 copy-start.4
  17.6 0.0 copy-start
  17.6 0.0 all-gather.5.cloned.1.call-start
  17.6 11.2 %convolution_convert_fusion = bf16[512,512]{0,1:T(8,128)(2,1)} fusion(bf16[512,8192]{1,0:T(8,128)(2,1)} %param.8, bf16[8192,512]{1,0:T(8,128)(2,1)} %param.10), kind=kOutput, calls=%fused_computation.12 | convolution fusion | flops 4295229440 | bytes 17301504 | tf_op jit(solution)/shard_map/dot_general | solution.py:31
  28.8 0.0 all-gather.5.cloned.1.call-update
  28.8 0.0 all-gather.11.cloned.1.call-start
  28.9 0.6 all-gather.9.cloned.1.call-done
  29.5 0.1 all-gather.11.cloned.1.call-update
  29.6 0.2 all-gather.7.cloned.1.call-start
  29.8 11.4 %all-gather.5.cloned.1.call-done = bf16[1024,4,128]{0,2,1:T(8,128)(2,1)} async-done(((bf16[512,4,128]{0,2,1:T(8,128)(2,1)}), bf16[1024,4,128]{0,2,1:T(8,128)(2,1)}) %all-gather.5.cloned.1.call-update) | async-done | bytes 1048592 | tf_op jit(solution)/shard_map/all_gather | solution.py:76
  41.2 0.0 all-gather.7.cloned.1.call-update
  41.3 0.0 copy-done.1
  41.3 0.0 copy-done.2
  41.3 0.0 copy-done.4
  41.3 0.1 select_reduce_fusion.1
  41.4 0.1 dynamic_slice.7
  41.5 0.1 dynamic_slice.6
  41.6 0.1 add_bitcast_fusion
  41.7 0.0 copy-done
  41.7 0.2 reshape.125
  41.9 3.7 %compare_and_fusion = pred[128,8192]{0,1:T(8,128)(4,1)S(1)} fusion(s32[128]{0:T(128)S(1)} %dynamic_slice.7, s32[128]{0:T(128)S(1)} %dynamic_slice.6, s32[8192]{0:T(1024)S(1)} %bitcast.54), kind=kLoop, calls=%fused_computation.10 | loop fusion | flops 3145728 | bytes 1082368 | tf_op jit(solution)/shard_map/and | solution.py:42
  45.6 123.4 %all-gather.11.cloned.1.call-done = bf16[8192,4,128]{2,0,1:T(8,128)(2,1)} async-done(((bf16[1024,4,128]{2,0,1:T(8,128)(2,1)}), bf16[8192,4,128]{2,0,1:T(8,128)(2,1)}) %all-gather.11.cloned.1.call-update) | async-done | bytes 8388624 | tf_op jit(solution)/shard_map/all_gather | solution.py:79
  169.1 28.2 %fusion.2 = (f32[4,128,4]{1,2,0:T(4,128)S(1)}, f32[4,8192,128,4]{2,1,3,0:T(8,128)}) fusion(pred[128,8192]{0,1:T(8,128)(4,1)S(1)} %compare_and_fusion, bf16[128,4,4,128]{3,2,1,0:T(4,128)(2,1)S(1)} %reshape.125, bf16[8192,4,128]{2,0,1:T(8,128)(2,1)} %all-gather.11.cloned.1.call-done), kind=kOutput, calls=%fused_computation.4 | convolution fusion | flops 4345296896 | bytes 77078528 | tf_op jit(solution)/shard_map/npgd,mgd->gnpm/dot_general | solution.py:39
  197.3 21.4 %fusion = f32[4,128,4]{1,2,0:T(4,128)S(1)} fusion(f32[4,8192,128,4]{2,1,3,0:T(8,128)} %get-tuple-element.10, f32[4,128,4]{1,2,0:T(4,128)S(1)} %get-tuple-element.9, pred[128,8192]{0,1:T(8,128)(4,1)S(1)} %compare_and_fusion), kind=kLoop, calls=%fused_computation.2 | loop fusion | flops 67106816 | bytes 68173824 | tf_op jit(solution)/shard_map/reduce_sum | solution.py:50
  218.7 75.1 %all-gather.7.cloned.1.call-done = bf16[8192,4,128]{0,2,1:T(8,128)(2,1)} async-done(((bf16[1024,4,128]{0,2,1:T(8,128)(2,1)}), bf16[8192,4,128]{0,2,1:T(8,128)(2,1)}) %all-gather.7.cloned.1.call-update) | async-done | bytes 8388624 | tf_op jit(solution)/shard_map/all_gather | solution.py:80
  293.8 27.0 %fusion.19 = bf16[128,4,4,128]{0,3,1,2:T(8,128)(2,1)S(1)} fusion(f32[4,8192,128,4]{2,1,3,0:T(8,128)} %get-tuple-element.10, f32[4,128,4]{1,2,0:T(4,128)S(1)} %get-tuple-element.9, pred[128,8192]{0,1:T(8,128)(4,1)S(1)} %compare_and_fusion, bf16[8192,4,128]{0,2,1:T(8,128)(2,1)} %all-gather.7.cloned.1.call-done, f32[128,4,4]{0,1,2:T(4,128)S(1)} %bitcast.55), kind=kOutput, calls=%fused_computation.14 | convolution fusion | flops 4362600448 | bytes 77086720 | tf_op jit(solution)/shard_map/gnpm,mgd->npgd/dot_general | solution.py:51
  320.8 1.2 copy.21
  (6 shorter events, 0.1 us)
Async XLA Ops:
  6.5 9.8 %copy-start.3 = (f32[128]{0:T(128)S(1)}, f32[128]{0:T(128)}, u32[]{:S(2)}) copy-start(f32[128]{0:T(128)} %param.11) | copy-start | bytes 1540
  6.5 22.9 %all-gather.9.cloned.1.call-start = ((), (), s32[]{:S(2)}) async-start(), calls=%async_computation.2 | async-start | bytes 1572864 | tf_op jit(solution)/shard_map/all_gather | solution.py:75
  17.5 23.7 %copy-start.1 = (s32[1024]{0:T(1024)S(1)}, s32[1024]{0:T(1024)}, u32[]{:S(2)}) copy-start(s32[1024]{0:T(1024)} %param.14) | copy-start | bytes 12292
  17.6 23.7 %copy-start.2 = (s32[1024]{0:T(1024)S(1)}, s32[1024]{0:T(1024)}, u32[]{:S(2)}) copy-start(s32[1024]{0:T(1024)} %param.15) | copy-start | bytes 12292
  17.6 23.7 %copy-start.4 = (s32[32]{0:T(128)S(1)}, s32[32]{0:T(128)}, u32[]{:S(2)}) copy-start(s32[32]{0:T(128)} %param.13) | copy-start | bytes 388
  17.6 24.1 %copy-start = (bf16[128,4,512]{2,1,0:T(4,128)(2,1)S(1)}, bf16[128,4,512]{2,1,0:T(4,128)(2,1)}, u32[]{:S(2)}) copy-start(bf16[128,4,512]{2,1,0:T(4,128)(2,1)} %param.12) | copy-start | bytes 1572868
  17.6 23.6 %all-gather.5.cloned.1.call-start = ((), (), s32[]{:S(2)}) async-start(), calls=%async_computation | async-start | bytes 1572864 | tf_op jit(solution)/shard_map/all_gather | solution.py:76
  28.8 140.3 %all-gather.11.cloned.1.call-start = ((), (), s32[]{:S(2)}) async-start(), calls=%async_computation.3 | async-start | bytes 9437184 | tf_op jit(solution)/shard_map/all_gather | solution.py:79
  29.6 264.2 %all-gather.7.cloned.1.call-start = ((), (), s32[]{:S(2)}) async-start(), calls=%async_computation.1 | async-start | bytes 9437184 | tf_op jit(solution)/shard_map/all_gather | solution.py:80
Sparse Core Ops, SparseCore 0:
  17.7 11.7 all-gather.8
  31.0 10.1 all-gather.4
  43.4 125.6 all-gather.10
  171.1 122.6 all-gather.6
where the time goes:
time: 329 us
  waiting for transfers between devices  211 us (64%)
  matrix products  75.8 us (23%)
  other arithmetic  26.5 us (8%)
  between operations  13.3 us (4%)
    all_gather x1, waiting for transfers between devices, body(): lax.all_gather(pair_keys, 'blk', axis=0, tiled=True)  123 us
    all_gather x1, waiting for transfers between devices, body(): lax.all_gather(pair_values, 'blk', axis=0, tiled=True)  75.1 us
    dot_general x1, matrix products, masked_scores(): jnp.einsum('npgd,mgd->gnpm', query_block, key_block, preferred_element_ty...  28.2 us
    dot_general x1, matrix products, weighted_sum(): jnp.einsum('gnpm,mgd->npgd', weights.astype(jnp.bfloat16), value_block, p...  27 us
    reduce_sum x1, other arithmetic, weighted_sum(): denominator = jnp.sum(weights, axis=3)  21.4 us
    all_gather x1, waiting for transfers between devices, body(): lax.all_gather(value_block, 'section', axis=0, tiled=True)  11.4 us
    dot_general x1, matrix products, make_tables(): jnp.dot(projected, value_weight, preferred_element_type=jnp.float32)  11.2 us
    dot_general x1, matrix products, make_tables(): jnp.dot(projected, key_weight, preferred_element_type=jnp.float32)  9.47 us
  transfers between devices with their start and end apart: 4, of which 4 were waited for; matrix products, arithmetic and copies ran while one was open for 20% of the time, Pallas kernels for 0%

commit v1 on v0

--- a/solution.py
+++ b/solution.py
@@ -5,6 +5,27 @@
 
 HD = 128
 FRAMES = 32
+
+
+def ring_gather(x, axis, dim):
+    peers, index, width = (lax.axis_size(axis), lax.axis_index(axis), x.shape[dim])
+    ahead = [(i, (i + 1) % peers) for i in range(peers)]
+    behind = [(i, (i - 1) % peers) for i in range(peers)]
+    out = jnp.zeros((*x.shape[:dim], peers * width, *x.shape[dim + 1 :]), x.dtype)
+    out = lax.dynamic_update_slice_in_dim(out, x, index * width, axis=dim)
+    from_left = from_right = x
+    half = peers // 2
+    for hop in range(1, half + 1):
+        from_left = lax.ppermute(from_left, axis, ahead)
+        out = lax.dynamic_update_slice_in_dim(
+            out, from_left, (index - hop) % peers * width, axis=dim
+        )
+        if hop < peers - half:
+            from_right = lax.ppermute(from_right, axis, behind)
+            out = lax.dynamic_update_slice_in_dim(
+                out, from_right, (index + hop) % peers * width, axis=dim
+            )
+    return out
 
 
 def span_bounds(frame_tokens, span_first, span_count):
@@ -77,7 +98,7 @@
     )
     all_keys, all_values = (
         lax.all_gather(pair_keys, "blk", axis=0, tiled=True),
-        lax.all_gather(pair_values, "blk", axis=0, tiled=True),
+        ring_gather(pair_values, "blk", 0),
     )
     block_ids = jnp.arange(block_count, dtype=jnp.int32)
     key_positions = (

time: 329 us -> 366 us (1.11)
  starting transfers between devices: 0.3 us -> 38.4 us
  waiting for transfers between devices: 211 us -> 190 us
  local copies, waits for them, and re-layouts: 1.94 us -> 22.9 us
    ppermute x0 -> x7, waiting for transfers between devices: none -> 177 us  [the longest x4 177 us: ring_gather(): from_left = lax.ppermute(from_left, axis, ahead)]
    all_gather x1, waiting for transfers between devices: 123 us -> 0.01 us  [body(): lax.all_gather(pair_keys, 'blk', axis=0, tiled=True)]
    all_gather x1 -> x0, waiting for transfers between devices: 75.1 us -> none  [body(): lax.all_gather(pair_values, 'blk', axis=0, tiled=True)]
    ppermute x0 -> x7, starting transfers between devices: none -> 38.4 us  [the longest x3 29.2 us: ring_gather(): from_right = lax.ppermute(from_right, axis, behind)]
    dynamic_update_slice x0 -> x8, local copies, waits for them, and re-layouts: none -> 14.7 us  [the longest x4 7.97 us: ring_gather(): lax.dynamic_update_slice_in_dim(out, from_left, (index - hop) % peers * w...]
    broadcast_in_dim x0 -> x1, local copies, waits for them, and re-layouts: none -> 4.33 us  [ring_gather(): jnp.zeros((*x.shape[:dim], peers * width, *x.shape[dim + 1:]), x.dtype)]
  transfers between devices with their start and end apart: 4 -> 10, of which waited for: 4 -> 6; matrix products, arithmetic and copies ran while one was open for 20% -> 10% of each run, Pallas kernels for 0% -> 0%
where the time goes in v1:
time: 366 us
  waiting for transfers between devices  190 us (52%)
  matrix products  74.8 us (20%)
  starting transfers between devices  38.4 us (10%)
  other arithmetic  26.3 us (7%)
  local copies, waits for them, and re-layouts  22.9 us (6%)
  between operations  13.4 us (4%)
    ppermute x4, waiting for transfers between devices, ring_gather(): from_left = lax.ppermute(from_left, axis, ahead)  177 us
    ppermute x3, starting transfers between devices, ring_gather(): from_right = lax.ppermute(from_right, axis, behind)  29.2 us
    dot_general x1, matrix products, masked_scores(): jnp.einsum('npgd,mgd->gnpm', query_block, key_block, preferred_element_ty...  27.3 us
    dot_general x1, matrix products, weighted_sum(): jnp.einsum('gnpm,mgd->npgd', weights.astype(jnp.bfloat16), value_block, p...  26.9 us
    reduce_sum x1, other arithmetic, weighted_sum(): denominator = jnp.sum(weights, axis=3)  21.3 us
    all_gather x1, waiting for transfers between devices, body(): lax.all_gather(value_block, 'section', axis=0, tiled=True)  11.7 us
    dot_general x1, matrix products, make_tables(): jnp.dot(projected, value_weight, preferred_element_type=jnp.float32)  11.1 us
    dot_general x1, matrix products, make_tables(): jnp.dot(projected, key_weight, preferred_element_type=jnp.float32)  9.47 us
  transfers between devices with their start and end apart: 10, of which 6 were waited for; matrix products, arithmetic and copies ran while one was open for 10% of the time, Pallas kernels for 0%

profile of v1, /device:TPU:0, one launch (start us, length us, event | category | flops | bytes accessed | tf_op | source)
XLA Modules:
  0.0 365.7 jit_solution(6911607863355597410)
XLA Ops:
  6.5 9.5 %multiply_reduce_fusion = (f32[512,4]{0,1:T(4,128)S(1)}, f32[512,512]{0,1:T(8,128)S(1)}) fusion(bf16[512,8192]{1,0:T(8,128)(2,1)} %param.8, bf16[8192,512]{1,0:T(8,128)(2,1)} %param.9), kind=kOutput, calls=%fused_computation.16 | convolution fusion | flops 4295489536 | bytes 17833984 | tf_op jit(solution)/shard_map/dot_general | solution.py:46
  16.0 0.3 copy.17
  16.4 1.1 multiply_convert_fusion
  17.5 0.0 all-gather.6.cloned.1.call-update
  17.5 0.0 copy-start.4
  17.6 0.0 copy-start.5
  17.6 0.0 copy-start.7
  17.6 0.0 all-gather.4.cloned.1.call-start
  17.6 11.1 %convolution_convert_fusion = bf16[512,512]{0,1:T(8,128)(2,1)} fusion(bf16[512,8192]{1,0:T(8,128)(2,1)} %param.8, bf16[8192,512]{1,0:T(8,128)(2,1)} %param.10), kind=kOutput, calls=%fused_computation.12 | convolution fusion | flops 4295229440 | bytes 17301504 | tf_op jit(solution)/shard_map/dot_general | solution.py:52
  28.7 0.0 all-gather.4.cloned.1.call-update
  28.8 0.0 all-gather.8.cloned.1.call-start
  28.8 0.6 all-gather.6.cloned.1.call-done
  29.4 0.1 all-gather.8.cloned.1.call-update
  29.5 11.7 %all-gather.4.cloned.1.call-done = bf16[1024,4,128]{0,2,1:T(8,128)(2,1)} async-done(((bf16[512,4,128]{0,2,1:T(8,128)(2,1)}), bf16[1024,4,128]{0,2,1:T(8,128)(2,1)}) %all-gather.4.cloned.1.call-update) | async-done | bytes 1048592 | tf_op jit(solution)/shard_map/all_gather | solution.py:97
  41.2 1.7 collective-permute-start
  43.0 3.0 collective-permute-start.1
  46.0 53.9 %collective-permute-done = bf16[1024,4,128]{0,2,1:T(8,128)(2,1)S(1)} collective-permute-done((bf16[1024,4,128]{0,2,1:T(8,128)(2,1)}, bf16[1024,4,128]{0,2,1:T(8,128)(2,1)S(1)}, u32[]{:S(2)}, u32[]{:S(2)}) %collective-permute-start) | collective-permute-done | bytes 1048608 | tf_op jit(solution)/shard_map/ppermute | solution.py:19
  99.9 2.4 collective-permute-start.2
  102.2 0.0 collective-permute-done.1
  102.2 2.8 collective-permute-start.3
  105.1 61.6 %collective-permute-done.2 = bf16[1024,4,128]{0,2,1:T(8,128)(2,1)} collective-permute-done((bf16[1024,4,128]{0,2,1:T(8,128)(2,1)S(1)}, bf16[1024,4,128]{0,2,1:T(8,128)(2,1)}, u32[]{:S(2)}, u32[]{:S(2)}) %collective-permute-start.2) | collective-permute-done | bytes 1048608 | tf_op jit(solution)/shard_map/ppermute | solution.py:19
  166.7 2.6 collective-permute-start.4
  169.3 0.0 copy-done.7
  169.3 0.1 select_reduce_fusion.1
  169.4 0.1 dynamic_slice.6
  169.5 0.1 dynamic_slice.7
  169.6 0.1 add_bitcast_fusion
  169.7 0.0 collective-permute-done.3
  169.7 23.4 %collective-permute-start.5 = (bf16[1024,4,128]{0,2,1:T(8,128)(2,1)}, bf16[1024,4,128]{0,2,1:T(8,128)(2,1)}, u32[]{:S(2)}, u32[]{:S(2)}) collective-permute-start(bf16[1024,4,128]{0,2,1:T(8,128)(2,1)} %collective-permute-done.3), channel_id=1, source_target_pairs={{0,14},{2,0},{4,2},{6,4},{8,6},{10,8},{12,10},{14,12},{1,15},{3,1}... | collective-permute-start | bytes 3145736 | tf_op jit(solution)/shard_map/ppermute | solution.py:24
  193.1 41.0 %collective-permute-done.4 = bf16[1024,4,128]{0,2,1:T(8,128)(2,1)} collective-permute-done((bf16[1024,4,128]{0,2,1:T(8,128)(2,1)}, bf16[1024,4,128]{0,2,1:T(8,128)(2,1)}, u32[]{:S(2)}, u32[]{:S(2)}) %collective-permute-start.4) | collective-permute-done | bytes 1048608 | tf_op jit(solution)/shard_map/ppermute | solution.py:19
  234.1 2.5 collective-permute-start.6
  236.6 3.7 %compare_and_fusion = pred[128,8192]{0,1:T(8,128)(4,1)S(1)} fusion(s32[128]{0:T(128)S(1)} %dynamic_slice.7, s32[128]{0:T(128)S(1)} %dynamic_slice.6, s32[8192]{0:T(1024)S(1)} %bitcast.54), kind=kLoop, calls=%fused_computation.10 | loop fusion | flops 3145728 | bytes 1082368 | tf_op jit(solution)/shard_map/and | solution.py:63
  240.4 2.0 reshape.125
  242.5 4.3 %broadcast_in_dim.26 = bf16[8192,4,128]{0,2,1:T(8,128)(2,1)} broadcast(bf16[]{:T(256)} %constant.61.clone.1), dimensions={} | broadcast | bytes 8388610 | tf_op jit(solution)/shard_map/broadcast_in_dim | solution.py:14
  246.8 1.1 constant_dynamic-update-slice_fusion.7
  247.9 1.1 constant_dynamic-update-slice_fusion.6
  248.9 1.1 constant_dynamic-update-slice_fusion.5
  250.0 2.3 constant_dynamic-update-slice_fusion.4
  252.3 2.3 constant_dynamic-update-slice_fusion.3
  254.6 2.3 constant_dynamic-update-slice_fusion.2
  256.9 0.0 collective-permute-done.5
  256.9 2.3 constant_dynamic-update-slice_fusion.1
  259.2 20.9 %collective-permute-done.6 = bf16[1024,4,128]{0,2,1:T(8,128)(2,1)} collective-permute-done((bf16[1024,4,128]{0,2,1:T(8,128)(2,1)}, bf16[1024,4,128]{0,2,1:T(8,128)(2,1)}, u32[]{:S(2)}, u32[]{:S(2)}) %collective-permute-start.6) | collective-permute-done | bytes 1048608 | tf_op jit(solution)/shard_map/ppermute | solution.py:19
  280.1 2.3 constant_dynamic-update-slice_fusion
  282.5 27.3 %fusion.2 = (f32[4,128,4]{1,2,0:T(4,128)S(1)}, f32[4,8192,128,4]{2,1,3,0:T(8,128)}) fusion(pred[128,8192]{0,1:T(8,128)(4,1)S(1)} %compare_and_fusion, bf16[128,4,4,128]{3,2,1,0:T(4,128)(2,1)S(1)} %copy-done.3, bf16[8192,4,128]{2,0,1:T(8,128)(2,1)} %all-gather.8.cloned.1.call-done), kind=kOutput, calls=%fused_computation.4 | convolution fusion | flops 4345296896 | bytes 77078528 | tf_op jit(solution)/shard_map/npgd,mgd->gnpm/dot_general | solution.py:60
  309.8 21.3 %fusion = f32[4,128,4]{1,2,0:T(4,128)S(1)} fusion(f32[4,8192,128,4]{2,1,3,0:T(8,128)} %get-tuple-element.10, f32[4,128,4]{1,2,0:T(4,128)S(1)} %get-tuple-element.9, pred[128,8192]{0,1:T(8,128)(4,1)S(1)} %compare_and_fusion), kind=kLoop, calls=%fused_computation.2 | loop fusion | flops 67106816 | bytes 68173824 | tf_op jit(solution)/shard_map/reduce_sum | solution.py:71
  331.0 26.9 %fusion.19 = bf16[128,4,4,128]{0,3,1,2:T(8,128)(2,1)S(1)} fusion(f32[4,8192,128,4]{2,1,3,0:T(8,128)} %get-tuple-element.10, f32[4,128,4]{1,2,0:T(4,128)S(1)} %get-tuple-element.9, pred[128,8192]{0,1:T(8,128)(4,1)S(1)} %compare_and_fusion, bf16[8192,4,128]{0,2,1:T(8,128)(2,1)} %constant_dynamic-update-slice_fusion, f32[128,4,4]{0,1,2:T(4,128)S(1)} %bitcast.55), kind=kOutput, calls=%fused_computation.14 | convolution fusion | flops 4362600448 | bytes 77086720 | tf_op jit(solution)/shard_map/gnpm,mgd->npgd/dot_general | solution.py:72
  358.0 1.2 copy.21
  (20 shorter events, 0.1 us)
Async XLA Ops:
  6.5 9.8 %copy-start.6 = (f32[128]{0:T(128)S(1)}, f32[128]{0:T(128)}, u32[]{:S(2)}) copy-start(f32[128]{0:T(128)} %param.11) | copy-start | bytes 1540
  6.5 22.9 %all-gather.6.cloned.1.call-start = ((), (), s32[]{:S(2)}) async-start(), calls=%async_computation.1 | async-start | bytes 1572864 | tf_op jit(solution)/shard_map/all_gather | solution.py:96
  17.5 151.7 %copy-start.4 = (s32[1024]{0:T(1024)S(1)}, s32[1024]{0:T(1024)}, u32[]{:S(2)}) copy-start(s32[1024]{0:T(1024)} %param.14) | copy-start | bytes 12292
  17.6 151.7 %copy-start.5 = (s32[1024]{0:T(1024)S(1)}, s32[1024]{0:T(1024)}, u32[]{:S(2)}) copy-start(s32[1024]{0:T(1024)} %param.15) | copy-start | bytes 12292
  17.6 151.7 %copy-start.7 = (s32[32]{0:T(128)S(1)}, s32[32]{0:T(128)}, u32[]{:S(2)}) copy-start(s32[32]{0:T(128)} %param.13) | copy-start | bytes 388
  17.6 23.6 %all-gather.4.cloned.1.call-start = ((), (), s32[]{:S(2)}) async-start(), calls=%async_computation | async-start | bytes 1572864 | tf_op jit(solution)/shard_map/all_gather | solution.py:97
  28.8 253.7 %all-gather.8.cloned.1.call-start = ((), (), s32[]{:S(2)}) async-start(), calls=%async_computation.2 | async-start | bytes 9437184 | tf_op jit(solution)/shard_map/all_gather | solution.py:100
  41.2 205.6 %copy-start = (bf16[1024,4,128]{0,2,1:T(8,128)(2,1)S(1)}, bf16[1024,4,128]{0,2,1:T(8,128)(2,1)}, u32[]{:S(2)}) copy-start(bf16[1024,4,128]{0,2,1:T(8,128)(2,1)} %all-gather.4.cloned.1.call-done) | copy-start | bytes 3145732
  41.2 58.6 %collective-permute-start = (bf16[1024,4,128]{0,2,1:T(8,128)(2,1)}, bf16[1024,4,128]{0,2,1:T(8,128)(2,1)S(1)}, u32[]{:S(2)}, u32[]{:S(2)}) collective-permute-start(bf16[1024,4,128]{0,2,1:T(8,128)(2,1)} %all-gather.4.cloned.1.call-done), channel_id=1, source_target_pairs={{0,2},{2,4},{4,6},{6,8},{8,10},{10,12},{12,14},{14,0},{1,3},{3,5},... | collective-permute-start | bytes 3145736 | tf_op jit(solution)/shard_map/ppermute | solution.py:19
  43.0 59.3 %collective-permute-start.1 = (bf16[1024,4,128]{0,2,1:T(8,128)(2,1)}, bf16[1024,4,128]{0,2,1:T(8,128)(2,1)S(1)}, u32[]{:S(2)}, u32[]{:S(2)}) collective-permute-start(bf16[1024,4,128]{0,2,1:T(8,128)(2,1)} %all-gather.4.cloned.1.call-done), channel_id=1, source_target_pairs={{0,14},{2,0},{4,2},{6,4},{8,6},{10,8},{12,10},{14,12},{1,15},{3,1}... | collective-permute-start | bytes 3145736 | tf_op jit(solution)/shard_map/ppermute | solution.py:24
  99.9 66.8 %collective-permute-start.2 = (bf16[1024,4,128]{0,2,1:T(8,128)(2,1)S(1)}, bf16[1024,4,128]{0,2,1:T(8,128)(2,1)}, u32[]{:S(2)}, u32[]{:S(2)}) collective-permute-start(bf16[1024,4,128]{0,2,1:T(8,128)(2,1)S(1)} %collective-permute-done), channel_id=1, source_target_pairs={{0,2},{2,4},{4,6},{6,8},{8,10},{10,12},{12,14},{14,0},{1,3},{3,5},... | collective-permute-start | bytes 3145736 | tf_op jit(solution)/shard_map/ppermute | solution.py:19
  102.2 134.3 %copy-start.1 = (bf16[1024,4,128]{0,2,1:T(8,128)(2,1)}, bf16[1024,4,128]{0,2,1:T(8,128)(2,1)S(1)}, u32[]{:S(2)}) copy-start(bf16[1024,4,128]{0,2,1:T(8,128)(2,1)S(1)} %collective-permute-done.1) | copy-start | bytes 3145732
  102.2 67.4 %collective-permute-start.3 = (bf16[1024,4,128]{0,2,1:T(8,128)(2,1)S(1)}, bf16[1024,4,128]{0,2,1:T(8,128)(2,1)}, u32[]{:S(2)}, u32[]{:S(2)}) collective-permute-start(bf16[1024,4,128]{0,2,1:T(8,128)(2,1)S(1)} %collective-permute-done.1), channel_id=1, source_target_pairs={{0,14},{2,0},{4,2},{6,4},{8,6},{10,8},{12,10},{14,12},{1,15},{3,1}... | collective-permute-start | bytes 3145736 | tf_op jit(solution)/shard_map/ppermute | solution.py:24
  166.7 67.4 %collective-permute-start.4 = (bf16[1024,4,128]{0,2,1:T(8,128)(2,1)}, bf16[1024,4,128]{0,2,1:T(8,128)(2,1)}, u32[]{:S(2)}, u32[]{:S(2)}) collective-permute-start(bf16[1024,4,128]{0,2,1:T(8,128)(2,1)} %collective-permute-done.2), channel_id=1, source_target_pairs={{0,2},{2,4},{4,6},{6,8},{8,10},{10,12},{12,14},{14,0},{1,3},{3,5},... | collective-permute-start | bytes 3145736 | tf_op jit(solution)/shard_map/ppermute | solution.py:19
  169.7 87.2 %collective-permute-start.5 = (bf16[1024,4,128]{0,2,1:T(8,128)(2,1)}, bf16[1024,4,128]{0,2,1:T(8,128)(2,1)}, u32[]{:S(2)}, u32[]{:S(2)}) collective-permute-start(bf16[1024,4,128]{0,2,1:T(8,128)(2,1)} %collective-permute-done.3), channel_id=1, source_target_pairs={{0,14},{2,0},{4,2},{6,4},{8,6},{10,8},{12,10},{14,12},{1,15},{3,1}... | collective-permute-start | bytes 3145736 | tf_op jit(solution)/shard_map/ppermute | solution.py:24
  234.1 46.0 %collective-permute-start.6 = (bf16[1024,4,128]{0,2,1:T(8,128)(2,1)}, bf16[1024,4,128]{0,2,1:T(8,128)(2,1)}, u32[]{:S(2)}, u32[]{:S(2)}) collective-permute-start(bf16[1024,4,128]{0,2,1:T(8,128)(2,1)} %collective-permute-done.4), channel_id=1, source_target_pairs={{0,2},{2,4},{4,6},{6,8},{8,10},{10,12},{12,14},{14,0},{1,3},{3,5},... | collective-permute-start | bytes 3145736 | tf_op jit(solution)/shard_map/ppermute | solution.py:19
  242.5 6.5 %copy-start.2 = (bf16[1024,4,128]{0,2,1:T(8,128)(2,1)S(1)}, bf16[1024,4,128]{0,2,1:T(8,128)(2,1)}, u32[]{:S(2)}) copy-start(bf16[1024,4,128]{0,2,1:T(8,128)(2,1)} %copy-done.1) | copy-start | bytes 3145732
  247.9 34.6 %copy-start.3 = (bf16[128,4,4,128]{3,2,1,0:T(4,128)(2,1)S(1)}, bf16[128,4,4,128]{3,2,1,0:T(4,128)(2,1)}, u32[]{:S(2)}) copy-start(bf16[128,4,4,128]{3,2,1,0:T(4,128)(2,1)} %reshape.125) | copy-start | bytes 1572868
Sparse Core Ops, SparseCore 0:
  17.7 11.7 all-gather.5
  31.0 10.1 all-gather.3
  43.4 227.8 all-gather.7
